TPU v7x, 256 devices: a whole 4x4x8 slice. The times are simulated.
256 devices in a mesh: site: 16 (over z_hi, y, core), blk: 16 (over z_lo, x).
Axes of the slice: x: 4, y: 4, z: 8 (z_hi: 2, z_lo: 4; z = z_hi * 4 + z_lo), core: 2. Of those that a mesh axis runs over, the one named last changes fastest.
Arguments:
- corner: bfloat16 [16, 96, 128, 128], P('site', 'blk')
- bcorner: bfloat16 [2, 16, 96, 128, 128], P(None, 'site', 'blk'), may hold values from -6 to 6
- edge: bfloat16 [16, 96, 128, 2304], P('site', 'blk'), may hold values from -0.5 to 0.5
- bedge: bfloat16 [16, 96, 128, 2304], P('site', 'blk'), may hold values from -0.5 to 0.5
- proj: bfloat16 [16, 96, 2304, 128], P('site', 'blk'), may hold values from -0.125 to 0.125
- joining: int32 [16, 96], P('site'), may hold values from 0 to 95, as said below
- momentum: float32 [1], replicated, may hold values from 0.5 to 2.5
Outputs:
- new_corner: bfloat16 [16, 96, 128, 128], P('site', 'blk')
- new_bcorner: bfloat16 [2, 16, 96, 128, 128], P(None, 'site', 'blk')
- momentum_sum: float32 [2, 96, 128, 128], P(None, 'blk', 'site')
Inputs may be any that keep to these rules, and one draw needn't show every extreme that they name: Each row of joining is a permutation of the 96 slots. The 6 new slots of one blk device take their blocks from the slots of at most 3 blk devices, exactly 2 from each of them.
All inputs are finite; a program needn't handle non-finite values. Where the computation divides by a largest or mean magnitude, that divisor is 1e-20 or more.
Results may differ from a plain program's by a relative error of at most 0.024.
Values may be sent and summed in bfloat16 or wider, within the bound.
A program may use at most 128 MiB of HBM per device.

v0:
```python
import jax
import jax.numpy as jnp
from jax import lax
from jax.sharding import PartitionSpec as P

epsilon = 1e-06


def shifted(block, axis, distance):
    devices = range(lax.axis_size(axis))
    route = [((i - distance) % len(devices), i) for i in devices]
    return lax.ppermute(block, axis, route)


def product(left, right):
    return jnp.einsum("jmn,jnk->jmk", left, right, preferred_element_type=jnp.float32)


def per_device(corner, bcorner, edge, bedge, proj, joining, momentum):
    per_dev = corner.shape[1]
    my_blk = lax.axis_index("blk")
    my_site = lax.axis_index("site")
    left_corner, left_bcorner = shifted((corner, bcorner), "site", 1)
    corner_here = left_corner[0]
    column = edge[0]
    bcolumn = bedge[0]
    project = proj[0]
    enlarged = product(corner_here, column).astype(jnp.bfloat16)
    real_term = product(left_bcorner[0, 0], column)
    imag_term = product(left_bcorner[1, 0], column)
    inserted = product(corner_here, bcolumn)
    angle = momentum[0] * my_site.astype(jnp.float32)
    cosine = jnp.cos(angle)
    sine = jnp.sin(angle)
    excited_re = (cosine * real_term - sine * imag_term + inserted).astype(jnp.bfloat16)
    excited_im = (sine * real_term + cosine * imag_term).astype(jnp.bfloat16)
    projected = jnp.stack(
        [
            product(enlarged, project).astype(jnp.bfloat16),
            product(excited_re, project).astype(jnp.bfloat16),
            product(excited_im, project).astype(jnp.bfloat16),
        ],
        axis=1,
    )
    local_peak = jnp.max(jnp.abs(projected[:, 0].astype(jnp.float32)))
    peak = lax.pmax(local_peak, "blk")
    sources = lax.dynamic_slice_in_dim(joining[0], my_blk * per_dev, per_dev)
    piece = lax.all_gather(projected, "blk", axis=0, tiled=True)
    picks = (sources[:, None] == jnp.arange(piece.shape[0], dtype=jnp.int32)[None, :]).astype(
        jnp.bfloat16
    )
    routed = jnp.einsum("it,txmn->ixmn", picks, piece, preferred_element_type=jnp.float32)
    scaled = routed / (peak + epsilon)
    new_corner = scaled[:, 0].astype(jnp.bfloat16)
    new_b = jnp.stack([scaled[:, 1], scaled[:, 2]], axis=0).astype(jnp.bfloat16)
    summed = lax.psum_scatter(
        new_b.astype(jnp.float32).astype(jnp.bfloat16), "site", scatter_dimension=2, tiled=True
    ).astype(jnp.float32)
    return (new_corner[None], new_b[:, None], summed)


def solution(mesh):
    in_specs = (
        P("site", "blk", None, None),
        P(None, "site", "blk", None, None),
        P("site", "blk", None, None),
        P("site", "blk", None, None),
        P("site", "blk", None, None),
        P("site", None),
        P(),
    )
    out_specs = (
        P("site", "blk", None, None),
        P(None, "site", "blk", None, None),
        P(None, "blk", "site", None),
    )
    return jax.shard_map(
        per_device, mesh=mesh, in_specs=in_specs, out_specs=out_specs, check_vma=False
    )
```

profile of v0, /device:TPU:1, one launch (start us, length us, event | category | flops | bytes accessed | tf_op | source)
XLA Modules:
  0.0 361.1 jit_solution(6874294399947471244)
XLA Ops:
  7.2 0.0 copy-start
  7.2 0.0 all-gather.2.cloned.1.call-start
  7.2 2.8 collective-permute-start
  10.0 0.1 collective-permute-start.1
  10.9 2.0 collective-permute-done
  12.9 0.0 copy-done
  12.9 5.4 %abs_reduce_fusion = (f32[]{:T(128)}, bf16[6,128,128]{2,1,0:T(8,128)(2,1)}) fusion(bf16[1,6,2304,128]{3,2,1,0:T(8,128)(2,1)} %param.11, bf16[1,6,128,2304]{3,2,1,0:T(8,128)(2,1)S(1)} %copy-done, bf16[1,6,128,128]{3,2,1,0:T(8,128)(2,1)} %collective-permute-done), kind=kOutput, calls=%fused_computation.34 | convolution fusion | flops 908132352 | bytes 7471108 | tf_op jit(solution)/shard_map/jmn,jnk->jmk/dot_general | solution.py:16
  18.3 0.0 collective-permute-done.1
  18.3 2.0 fusion.10
  20.3 0.0 copy-start.1
  20.3 2.2 fusion.12
  22.5 0.7 copy-done.1
  23.2 0.0 copy-start.2
  23.2 2.9 copy-done.2
  26.2 4.0 %fusion.43 = bf16[6,1,128,128]{3,2,0,1:T(8,128)(2,1)} fusion(bf16[1,6,2304,128]{3,2,1,0:T(8,128)(2,1)} %param.11, f32[6,128,2304]{2,1,0:T(8,128)S(1)} %fusion.10, f32[6,128,2304]{2,1,0:T(8,128)S(1)} %fusion.12, f32[]{:T(128)S(6)} %sin.3, f32[]{:T(128)S(6)} %cos.3), kind=kOutput, calls=%fused_computation.26 | convolution fusion | flops 460161024 | bytes 17891336 | tf_op jit(solution)/shard_map/jmn,jnk->jmk/dot_general | solution.py:16
  30.2 0.0 copy-start.3
  30.2 10.1 %fusion.38 = bf16[6,1,128,128]{3,2,0,1:T(8,128)(2,1)} fusion(bf16[1,6,2304,128]{3,2,1,0:T(8,128)(2,1)} %param.11, f32[6,128,2304]{2,1,0:T(8,128)} %copy-done.1, f32[6,128,2304]{2,1,0:T(8,128)} %copy-done.2, f32[]{:T(128)S(6)} %sin.3, f32[]{:T(128)S(6)} %cos.3, bf16[1,6,128,2304]{3,2,1,0:T(8,128)(2,1)} %param.10, ...), kind=kOutput, calls=%fused_computation.25 | convolution fusion | flops 914915328 | bytes 21626888 | tf_op jit(solution)/shard_map/jmn,jnk->jmk/dot_general | solution.py:16
  40.3 2.0 pad_maximum_fusion
  42.3 0.0 all-gather.2.cloned.1.call-update
  42.3 0.0 all-reduce.3.cloned.1.call-start
  42.4 0.0 copy-done.3
  42.4 0.1 dynamic-slice_bitcast_fusion
  42.5 39.0 %pmax.7 = f32[]{:T(128)} all-reduce(f32[]{:T(128)} %get-tuple-element.14), channel_id=1, replica_groups=mesh['site'=16,'blk'=16] {'blk'}, use_global_device_ids=true, to_apply=%region_1.0 | all-reduce | flops 1 | bytes 8 | tf_op jit(solution)/shard_map/pmax | solution.py:46
  82.2 85.8 %all-gather.2.cloned.1.call-done = bf16[96,3,128,128]{3,2,0,1:T(8,128)(2,1)} async-done(((bf16[6,3,128,128]{3,2,0,1:T(8,128)(2,1)}), bf16[96,3,128,128]{3,2,0,1:T(8,128)(2,1)}) %all-gather.2.cloned.1.call-update) | async-done | bytes 9437200 | tf_op jit(solution)/shard_map/all_gather | solution.py:48
  167.9 8.8 %fusion.46 = bf16[6,3,128,128]{3,0,2,1:T(8,128)(2,1)S(1)} fusion(bf16[96,3,128,128]{3,2,0,1:T(8,128)(2,1)} %all-gather.2.cloned.1.call-done, f32[]{:T(128)S(6)} %add.17, s32[6]{0:T(128)S(1)} %dynamic-slice_bitcast_fusion), kind=kOutput, calls=%fused_computation.27 | convolution fusion | flops 57213504 | bytes 10027036 | tf_op jit(solution)/shard_map/it,txmn->ixmn/dot_general | solution.py:52
  176.7 0.0 copy-start.4
  176.7 1.0 fusion.54
  177.7 0.1 pad_maximum_fusion.2
  177.8 1.4 copy.15
  179.2 0.0 all-reduce.3.cloned.1.call-update
  179.2 0.0 copy-done.4
  179.2 0.6 dynamic-slice.1
  180.5 1.2 pad_maximum_fusion.1
  181.6 0.8 copy.17
  182.4 1.7 copy.16
  184.1 168.7 %all-reduce.3.cloned.1.call-done = bf16[2,6,128,128]{3,0,1,2:T(2,128)(2,1)} async-done(((bf16[2,6,128,128]{3,0,1,2:T(2,128)(2,1)}), bf16[2,6,128,128]{3,0,1,2:T(2,128)(2,1)}) %all-reduce.3.cloned.1.call-update) | async-done | bytes 393232
  352.8 0.8 dynamic-slice_convert_fusion
  353.6 0.6 copy.18
Async XLA Ops:
  7.2 5.8 %copy-start = (bf16[1,6,128,2304]{3,2,1,0:T(8,128)(2,1)S(1)}, bf16[1,6,128,2304]{3,2,1,0:T(8,128)(2,1)}, u32[]{:S(2)}) copy-start(bf16[1,6,128,2304]{3,2,1,0:T(8,128)(2,1)} %param.9) | copy-start | bytes 10616836
  7.2 160.7 %all-gather.2.cloned.1.call-start = ((), (), s32[]{:S(2)}) async-start(), calls=%async_computation | async-start | bytes 10027008 | tf_op jit(solution)/shard_map/all_gather | solution.py:48
  7.2 5.7 %collective-permute-start = (bf16[1,6,128,128]{3,2,1,0:T(8,128)(2,1)}, bf16[1,6,128,128]{3,2,1,0:T(8,128)(2,1)}, u32[]{:S(2)}, u32[]{:S(2)}) collective-permute-start(bf16[1,6,128,128]{3,2,1,0:T(8,128)(2,1)} %param.7), channel_id=1, source_target_pairs={{240,0},{0,16},{16,32},{32,48},{48,64},{64,80},{80,96},{96,112},{1... | collective-permute-start | bytes 589832 | tf_op jit(solution)/shard_map/ppermute | solution.py:12
  10.0 8.3 %collective-permute-start.1 = (bf16[2,1,6,128,128]{4,3,2,1,0:T(8,128)(2,1)}, bf16[2,1,6,128,128]{4,3,2,1,0:T(8,128)(2,1)}, u32[]{:S(2)}, u32[]{:S(2)}) collective-permute-start(bf16[2,1,6,128,128]{4,3,2,1,0:T(8,128)(2,1)} %param.8), channel_id=1, source_target_pairs={{240,0},{0,16},{16,32},{32,48},{48,64},{64,80},{80,96},{96,112},{1... | collective-permute-start | bytes 1179656 | tf_op jit(solution)/shard_map/ppermute | solution.py:12
  20.3 2.9 copy-start.1
  23.2 2.9 copy-start.2
  30.2 12.2 %copy-start.3 = (s32[1,96]{1,0:T(1,128)S(1)}, s32[1,96]{1,0:T(1,128)}, u32[]{:S(2)}) copy-start(s32[1,96]{1,0:T(1,128)} %param.12) | copy-start | bytes 1156
  42.3 310.5 %all-reduce.3.cloned.1.call-start = ((), (), s32[]{:S(2)}) async-start(), calls=%async_computation.1 | async-start | bytes 786432
  176.7 2.5 copy-start.4
Sparse Core Ops, SparseCore 0:
  42.4 125.4 all-gather.1
  179.3 173.4 all-reduce.2
where the time goes:
time: 361 us
  waiting for transfers between devices  257 us (71%)
  blocking collectives  39 us (11%)
  matrix products  32.5 us (9%)
  between operations  16.2 us (4%)
  local copies, waits for them, and re-layouts  9.75 us (3%)
  other arithmetic  4.03 us (1%)
    unnamed x3, waiting for transfers between devices  169 us
    all_gather x1, waiting for transfers between devices, per_device(): piece = lax.all_gather(projected, 'blk', axis=0, tiled=True)  85.8 us
    pmax x1, blocking collectives, per_device(): peak = lax.pmax(local_peak, 'blk')  39 us
    dot_general x5, matrix products, product(): jnp.einsum('jmn,jnk->jmk', left, right, preferred_element_type=jnp.float32)  23.7 us
    dot_general x1, matrix products, per_device(): jnp.einsum('it,txmn->ixmn', picks, piece, preferred_element_type=jnp.floa...  8.79 us
    unnamed x14, local copies, waits for them, and re-layouts  7.33 us
  transfers between devices with their start and end apart: 4, of which 3 were waited for; matrix products, arithmetic and copies ran while one was open for 3% of the time, Pallas kernels for 0%

commit v1 on v0

--- a/solution.py
+++ b/solution.py
@@ -17,6 +17,12 @@
 
 
 def per_device(corner, bcorner, edge, bedge, proj, joining, momentum):
+
+    def _produce_indices(v0):
+        f_now = jnp.stack([v0 for _ in range(lax.axis_size("blk"))], axis=0)
+        outer = lax.all_to_all(f_now, "blk", split_axis=0, concat_axis=0)
+        return jnp.concatenate(outer, 0)
+
     per_dev = corner.shape[1]
     my_blk = lax.axis_index("blk")
     my_site = lax.axis_index("site")
@@ -45,7 +51,7 @@
     local_peak = jnp.max(jnp.abs(projected[:, 0].astype(jnp.float32)))
     peak = lax.pmax(local_peak, "blk")
     sources = lax.dynamic_slice_in_dim(joining[0], my_blk * per_dev, per_dev)
-    piece = lax.all_gather(projected, "blk", axis=0, tiled=True)
+    piece = _produce_indices(projected)
     picks = (sources[:, None] == jnp.arange(piece.shape[0], dtype=jnp.int32)[None, :]).astype(
         jnp.bfloat16
     )

time: 361 us -> 484 us (1.34)
  blocking collectives: 39 us -> 171 us
  waiting for transfers between devices: 257 us -> 233 us
  starting transfers between devices: 2.93 us -> 11.3 us
  local copies, waits for them, and re-layouts: 9.75 us -> 15.8 us
    pmax x1, blocking collectives: 39 us -> 171 us  [per_device(): peak = lax.pmax(local_peak, 'blk')]
    all_gather x1 -> x0, waiting for transfers between devices: 85.8 us -> none  [per_device(): piece = lax.all_gather(projected, 'blk', axis=0, tiled=True)]
    unnamed x3 -> x2, waiting for transfers between devices: 169 us -> 231 us
    all_to_all x0 -> x1, starting transfers between devices: none -> 8.36 us  [_produce_indices(): outer = lax.all_to_all(f_now, 'blk', split_axis=0, concat_axis=0)]
    another operation x0 -> x2, local copies, waits for them, and re-layouts: none -> 6.08 us  [the longest x1 6.04 us: _produce_indices(): f_now = jnp.stack([v0 for _ in range(lax.axis_size('blk'))], axis=0)]
  transfers between devices with their start and end apart: 4 -> 4, of which waited for: 3 -> 2; matrix products, arithmetic and copies ran while one was open for 3% -> 2% of each run, Pallas kernels for 0% -> 0%
where the time goes in v1:
time: 484 us
  waiting for transfers between devices  233 us (48%)
  blocking collectives  171 us (35%)
  matrix products  32.5 us (7%)
  between operations  16.2 us (3%)
  local copies, waits for them, and re-layouts  15.8 us (3%)
  starting transfers between devices  11.3 us (2%)
    unnamed x2, waiting for transfers between devices  231 us
    pmax x1, blocking collectives, per_device(): peak = lax.pmax(local_peak, 'blk')  171 us
    dot_general x5, matrix products, product(): jnp.einsum('jmn,jnk->jmk', left, right, preferred_element_type=jnp.float32)  23.7 us
  transfers between devices with their start and end apart: 4, of which 2 were waited for; matrix products, arithmetic and copies ran while one was open for 2% of the time, Pallas kernels for 0%

profile of v1, /device:TPU:1, one launch (start us, length us, event | category | flops | bytes accessed | tf_op | source)
XLA Modules:
  0.0 483.6 jit_solution(4408063963492632730)
XLA Ops:
  7.2 0.0 copy-start
  7.2 2.8 collective-permute-start
  9.9 0.1 collective-permute-start.1
  10.8 2.0 collective-permute-done
  12.9 0.0 copy-done
  12.9 5.4 %abs_reduce_fusion = (f32[]{:T(128)}, bf16[6,128,128]{2,1,0:T(8,128)(2,1)}) fusion(bf16[1,6,2304,128]{3,2,1,0:T(8,128)(2,1)} %param.11, bf16[1,6,128,2304]{3,2,1,0:T(8,128)(2,1)S(1)} %copy-done, bf16[1,6,128,128]{3,2,1,0:T(8,128)(2,1)} %collective-permute-done), kind=kOutput, calls=%fused_computation.34 | convolution fusion | flops 908132352 | bytes 7471108 | tf_op jit(solution)/shard_map/jmn,jnk->jmk/dot_general | solution.py:16
  18.3 0.0 collective-permute-done.1
  18.3 2.0 fusion.10
  20.3 0.0 copy-start.1
  20.3 2.2 fusion.12
  22.5 0.7 copy-done.1
  23.2 0.0 copy-start.2
  23.2 2.9 copy-done.2
  26.1 4.0 fusion.43
  30.1 10.1 %fusion.38 = bf16[6,1,128,128]{3,2,0,1:T(8,128)(2,1)} fusion(bf16[1,6,2304,128]{3,2,1,0:T(8,128)(2,1)} %param.11, f32[6,128,2304]{2,1,0:T(8,128)} %copy-done.1, f32[6,128,2304]{2,1,0:T(8,128)} %copy-done.2, f32[]{:T(128)S(6)} %sin.3, f32[]{:T(128)S(6)} %cos.3, bf16[1,6,128,2304]{3,2,1,0:T(8,128)(2,1)} %param.10, ...), kind=kOutput, calls=%fused_computation.25 | convolution fusion | flops 914915328 | bytes 21626888 | tf_op jit(solution)/shard_map/jmn,jnk->jmk/dot_general | solution.py:16
  40.2 1.2 pad_maximum_fusion
  41.5 6.0 %stack.45 = bf16[16,6,3,128,128]{4,3,2,1,0:T(8,128)(2,1)} broadcast(bf16[6,3,128,128]{3,2,1,0:T(8,128)(2,1)S(1)} %copy.19), dimensions={1,2,3,4} | broadcast | bytes 10027008 | tf_op jit(solution)/shard_map/stack | solution.py:22
  47.5 0.0 copy-start.3
  47.5 8.4 %all-to-all-start = ((bf16[16,6,3,128,128]{4,3,2,1,0:T(8,128)(2,1)}), bf16[16,6,3,128,128]{4,3,2,1,0:T(8,128)(2,1)}, u32[]{:S(2)}, u32[]{:S(2)}) async-start(bf16[16,6,3,128,128]{4,3,2,1,0:T(8,128)(2,1)} %stack.45), calls=%async_computation | async-start | bytes 18874368 | tf_op jit(solution)/shard_map/all_to_all | solution.py:23
  55.9 0.0 all-reduce.3.cloned.1.call-start
  55.9 0.0 copy-done.3
  56.0 0.1 dynamic-slice_bitcast_fusion
  56.0 171.3 %pmax.7 = f32[]{:T(128)} all-reduce(f32[]{:T(128)} %get-tuple-element.17), channel_id=1, replica_groups=mesh['site'=16,'blk'=16] {'blk'}, use_global_device_ids=true, to_apply=%region_1.0 | all-reduce | flops 1 | bytes 8 | tf_op jit(solution)/shard_map/pmax | solution.py:52
  228.0 0.0 all-to-all-done
  228.0 8.8 %fusion.46 = bf16[6,3,128,128]{3,0,2,1:T(8,128)(2,1)S(1)} fusion(bf16[96,3,128,128]{3,2,1,0:T(8,128)(2,1)} %bitcast.13, f32[]{:T(128)S(6)} %add.17, s32[6]{0:T(128)S(1)} %dynamic-slice_bitcast_fusion), kind=kOutput, calls=%fused_computation.27 | convolution fusion | flops 57213504 | bytes 10027036 | tf_op jit(solution)/shard_map/it,txmn->ixmn/dot_general | solution.py:58
  236.8 0.0 copy-start.4
  236.8 1.0 fusion.54
  237.7 0.1 pad_maximum_fusion.2
  237.9 1.4 copy.21
  239.2 0.0 all-reduce.3.cloned.1.call-update
  239.2 0.0 copy-done.4
  239.3 0.6 dynamic-slice.1
  240.5 1.2 pad_maximum_fusion.1
  241.7 0.8 copy.23
  242.5 1.7 copy.22
  244.1 231.2 %all-reduce.3.cloned.1.call-done = bf16[2,6,128,128]{3,0,1,2:T(2,128)(2,1)} async-done(((bf16[2,6,128,128]{3,0,1,2:T(2,128)(2,1)}), bf16[2,6,128,128]{3,0,1,2:T(2,128)(2,1)}) %all-reduce.3.cloned.1.call-update) | async-done | bytes 393232
  475.4 0.8 dynamic-slice_convert_fusion
  476.1 0.6 copy.24
  (1 shorter events, 0.0 us)
Async XLA Ops:
  7.2 5.7 %copy-start = (bf16[1,6,128,2304]{3,2,1,0:T(8,128)(2,1)S(1)}, bf16[1,6,128,2304]{3,2,1,0:T(8,128)(2,1)}, u32[]{:S(2)}) copy-start(bf16[1,6,128,2304]{3,2,1,0:T(8,128)(2,1)} %param.9) | copy-start | bytes 10616836
  7.2 5.7 %collective-permute-start = (bf16[1,6,128,128]{3,2,1,0:T(8,128)(2,1)}, bf16[1,6,128,128]{3,2,1,0:T(8,128)(2,1)}, u32[]{:S(2)}, u32[]{:S(2)}) collective-permute-start(bf16[1,6,128,128]{3,2,1,0:T(8,128)(2,1)} %param.7), channel_id=1, source_target_pairs={{240,0},{0,16},{16,32},{32,48},{48,64},{64,80},{80,96},{96,112},{1... | collective-permute-start | bytes 589832 | tf_op jit(solution)/shard_map/ppermute | solution.py:12
  9.9 8.3 %collective-permute-start.1 = (bf16[2,1,6,128,128]{4,3,2,1,0:T(8,128)(2,1)}, bf16[2,1,6,128,128]{4,3,2,1,0:T(8,128)(2,1)}, u32[]{:S(2)}, u32[]{:S(2)}) collective-permute-start(bf16[2,1,6,128,128]{4,3,2,1,0:T(8,128)(2,1)} %param.8), channel_id=1, source_target_pairs={{240,0},{0,16},{16,32},{32,48},{48,64},{64,80},{80,96},{96,112},{1... | collective-permute-start | bytes 1179656 | tf_op jit(solution)/shard_map/ppermute | solution.py:12
  20.3 2.9 copy-start.1
  23.2 2.9 copy-start.2
  47.5 8.4 %copy-start.3 = (s32[1,96]{1,0:T(1,128)S(1)}, s32[1,96]{1,0:T(1,128)}, u32[]{:S(2)}) copy-start(s32[1,96]{1,0:T(1,128)} %param.12) | copy-start | bytes 1156
  47.5 180.4 %all-to-all-start = ((bf16[16,6,3,128,128]{4,3,2,1,0:T(8,128)(2,1)}), bf16[16,6,3,128,128]{4,3,2,1,0:T(8,128)(2,1)}, u32[]{:S(2)}, u32[]{:S(2)}) async-start(bf16[16,6,3,128,128]{4,3,2,1,0:T(8,128)(2,1)} %stack.45), calls=%async_computation | async-start | bytes 18874368 | tf_op jit(solution)/shard_map/all_to_all | solution.py:23
  55.9 419.5 %all-reduce.3.cloned.1.call-start = ((), (), s32[]{:S(2)}) async-start(), calls=%async_computation.1 | async-start | bytes 786432
  236.8 2.5 copy-start.4
Sparse Core Ops, SparseCore 0:
  239.4 235.9 all-reduce.2
